TPU v7x, 32 devices: a whole 2x2x4 slice. The times are simulated.
32 devices in a mesh: pair: 2 (over x), seq: 4 (over z), head: 4 (over y, core).
Axes of the slice: x: 2, y: 2, z: 4, core: 2. Of those that a mesh axis runs over, the one named last changes fastest.
Arguments:
- resp_query: bfloat16 [2, 4, 256, 4096], P('pair', 'seq', None, 'head'), may hold values from -6 to 6
- resp_key: bfloat16 [2, 4, 256, 1024], P('pair', 'seq', None, 'head'), may hold values from -6 to 6
- resp_value: bfloat16 [2, 4, 256, 1024], P('pair', 'seq', None, 'head'), may hold values from -6 to 6
- direction: bfloat16 [2, 4, 256, 4096], P('pair', 'seq', None, 'head'), may hold values from -96 to 96
- ratio: float32 [2, 4, 256], P('pair', 'seq'), may hold values from -4.2 to 4.2
- lengths: int32 [2, 4], P('pair', 'seq'), may hold values from 1 to 256, 640 in all within a row
- partner: int32 [4], replicated, may hold values from 0 to 3, each once
- prompt_key: bfloat16 [1024, 1024], P('pair', 'head'), may hold values from -6 to 6
- prompt_value: bfloat16 [1024, 1024], P('pair', 'head'), may hold values from -6 to 6
Outputs:
- query_grad: bfloat16 [2, 4, 256, 4096], P('pair', 'seq', None, 'head')
- resp_key_grad: bfloat16 [2, 4, 256, 1024], P('pair', 'seq', None, 'head')
- resp_value_grad: bfloat16 [2, 4, 256, 1024], P('pair', 'seq', None, 'head')
- prompt_key_grad: bfloat16 [1024, 1024], P('pair', 'head')
- prompt_value_grad: bfloat16 [1024, 1024], P('pair', 'head')
Inputs may be any that keep to these rules, and one draw needn't show every extreme that they name: On each side the response lengths sum to 640, and the longest is 256. partner names each rejected response exactly once.
All inputs are finite; a program needn't handle non-finite values. No bound on the sum of `lengths` on one device may be relied on, other than what follows from the above.
Results may differ from a plain program's by a relative error of at most 0.03.
Values may be sent and summed in bfloat16 or wider, within the bound.
A program may use at most 64 MiB of HBM per device.

v0:
```python
from functools import partial
import math

import jax
import jax.numpy as jnp
from jax import lax
from jax.sharding import PartitionSpec as P

HEAD_DIM = 128


dpo_beta = 0.1
block_limit = 128


def block_pass(operands, first_row, length, prompt_rows, head_group, score_scale):
    rows_q, rows_g, key_rows, value_rows = operands
    scores = jnp.dot(rows_q, key_rows.T, preferred_element_type=jnp.float32) * score_scale
    row_pos = first_row + jnp.arange(rows_q.shape[0], dtype=jnp.int32) // head_group
    key_pos = jnp.arange(key_rows.shape[0], dtype=jnp.int32) - prompt_rows
    visible = (key_pos[None, :] < 0) | (key_pos[None, :] <= row_pos[:, None]) & (
        key_pos[None, :] < length
    )
    scores = jnp.where(visible, scores, -jnp.inf)
    row_max = jnp.max(scores, axis=1, keepdims=True)
    exponent = jnp.exp(scores - row_max)
    attn_prob = exponent / jnp.sum(exponent, axis=1, keepdims=True)
    prob_half = attn_prob.astype(jnp.bfloat16)
    attended = jnp.dot(prob_half, value_rows, preferred_element_type=jnp.float32).astype(
        jnp.bfloat16
    )
    row_delta = jnp.sum(
        rows_g.astype(jnp.float32) * attended.astype(jnp.float32), axis=1, keepdims=True
    )
    prob_grad = jnp.dot(rows_g, value_rows.T, preferred_element_type=jnp.float32)
    score_grad = (attn_prob * (prob_grad - row_delta)).astype(jnp.bfloat16)
    query_rows = (
        jnp.dot(score_grad, key_rows, preferred_element_type=jnp.float32) * score_scale
    ).astype(jnp.bfloat16)
    key_add = jnp.dot(score_grad.T, rows_q, preferred_element_type=jnp.float32) * score_scale
    value_add = jnp.dot(prob_half.T, rows_g, preferred_element_type=jnp.float32)
    return (query_rows, key_add, value_add)


def block_skip(operands):
    rows_q, rows_g, key_rows, value_rows = operands
    empty_keys = jnp.zeros((key_rows.shape[0], key_rows.shape[1]), jnp.float32)
    return (jnp.zeros_like(rows_q), empty_keys, empty_keys)


def shards(
    resp_query, resp_key, resp_value, direction, ratio, lengths, partner, prompt_key, prompt_value
):
    length = lengths[0, 0]
    resp_rows = resp_query.shape[2]
    positions = jnp.arange(resp_rows, dtype=jnp.int32)
    live_mask = positions < length
    own_sum = jnp.sum(jnp.where(live_mask, ratio[0, 0], 0.0))
    side_index = lax.axis_index("pair")
    seq_index = lax.axis_index("seq")
    response_count = partner.shape[0]
    response_ids = jnp.arange(response_count, dtype=jnp.int32)
    side_ids = jnp.arange(2, dtype=jnp.int32)
    owned = (side_ids[:, None] == side_index) & (response_ids[None, :] == seq_index)
    score_table = lax.psum(jnp.where(owned, own_sum, 0.0), ("pair", "seq"))
    matched = partner[:, None] == response_ids[None, :]
    partner_sums = jnp.sum(jnp.where(matched, score_table[1][None, :], 0.0), axis=1)
    pulled = jax.nn.sigmoid(-(dpo_beta * (score_table[0] - partner_sums)))
    chosen_weight = -jnp.sum(jnp.where(response_ids == seq_index, pulled, 0.0))
    rejected_weight = jnp.sum(jnp.where(partner == seq_index, pulled, 0.0))
    weight = jnp.where(side_index == 0, chosen_weight, rejected_weight)
    out_grads = jnp.where(
        live_mask[:, None], weight * direction[0, 0].astype(jnp.float32), 0.0
    ).astype(jnp.bfloat16)
    whole_key, whole_value = (
        lax.all_gather(prompt_key, "pair", axis=0, tiled=True),
        lax.all_gather(prompt_value, "pair", axis=0, tiled=True),
    )
    kv_local = resp_key.shape[3] // HEAD_DIM
    head_group = resp_query.shape[3] // resp_key.shape[3]
    prompt_rows = whole_key.shape[0]
    block_rows = min(block_limit, resp_rows)
    score_scale = 1.0 / math.sqrt(HEAD_DIM)
    query_heads, key_heads, value_heads, prompt_key_terms, prompt_value_terms = ([], [], [], [], [])
    for kv_index in range(kv_local):
        head_cols = slice(kv_index * head_group * HEAD_DIM, (kv_index + 1) * head_group * HEAD_DIM)
        key_cols = slice(kv_index * HEAD_DIM, (kv_index + 1) * HEAD_DIM)
        query_head = resp_query[0, 0][:, head_cols]
        grad_head = out_grads[:, head_cols]
        resp_k = resp_key[0, 0][:, key_cols]
        resp_v = resp_value[0, 0][:, key_cols]
        prompt_k = whole_key[:, key_cols]
        prompt_v = whole_value[:, key_cols]
        prompt_dk = jnp.zeros((prompt_rows, HEAD_DIM), jnp.float32)
        prompt_dv = jnp.zeros((prompt_rows, HEAD_DIM), jnp.float32)
        resp_dk = jnp.zeros((resp_rows, HEAD_DIM), jnp.float32)
        resp_dv = jnp.zeros((resp_rows, HEAD_DIM), jnp.float32)
        query_blocks = []
        for block_index in range(resp_rows // block_rows):
            first_row = block_index * block_rows
            end_row = first_row + block_rows
            key_rows = jnp.concatenate([prompt_k, resp_k[:end_row]], 0)
            value_rows = jnp.concatenate([prompt_v, resp_v[:end_row]], 0)
            rows_q = query_head[first_row:end_row].reshape(block_rows * head_group, HEAD_DIM)
            rows_g = grad_head[first_row:end_row].reshape(block_rows * head_group, HEAD_DIM)
            active = partial(
                block_pass,
                first_row=first_row,
                length=length,
                prompt_rows=prompt_rows,
                head_group=head_group,
                score_scale=score_scale,
            )
            query_rows, key_add, value_add = lax.cond(
                first_row < length, active, block_skip, (rows_q, rows_g, key_rows, value_rows)
            )
            query_blocks.append(query_rows)
            prompt_dk = prompt_dk + key_add[:prompt_rows]
            prompt_dv = prompt_dv + value_add[:prompt_rows]
            resp_dk = resp_dk.at[:end_row].add(key_add[prompt_rows:])
            resp_dv = resp_dv.at[:end_row].add(value_add[prompt_rows:])
        query_heads.append(
            jnp.concatenate(query_blocks, 0).reshape(resp_rows, head_group * HEAD_DIM)
        )
        key_heads.append(resp_dk.astype(jnp.bfloat16))
        value_heads.append(resp_dv.astype(jnp.bfloat16))
        prompt_key_terms.append(prompt_dk)
        prompt_value_terms.append(prompt_dv)
    prompt_terms = jnp.concatenate(prompt_key_terms + prompt_value_terms, 1)
    own_rows = prompt_key.shape[0]
    summed = lax.psum(prompt_terms, ("pair", "seq"))
    reduced = lax.dynamic_slice_in_dim(summed, side_index * own_rows, own_rows, 0).astype(
        jnp.bfloat16
    )
    key_width = kv_local * HEAD_DIM
    query_grad = jnp.concatenate(query_heads, 1)[None, None]
    resp_key_grad = jnp.concatenate(key_heads, 1)[None, None]
    resp_value_grad = jnp.concatenate(value_heads, 1)[None, None]
    prompt_key_grad = reduced[:, :key_width]
    prompt_value_grad = reduced[:, key_width:]
    return (query_grad, resp_key_grad, resp_value_grad, prompt_key_grad, prompt_value_grad)


def solution(mesh):
    in_specs = (
        P("pair", "seq", None, "head"),
        P("pair", "seq", None, "head"),
        P("pair", "seq", None, "head"),
        P("pair", "seq", None, "head"),
        P("pair", "seq", None),
        P("pair", "seq"),
        P(),
        P("pair", "head"),
        P("pair", "head"),
    )
    out_specs = (
        P("pair", "seq", None, "head"),
        P("pair", "seq", None, "head"),
        P("pair", "seq", None, "head"),
        P("pair", "head"),
        P("pair", "head"),
    )
    return jax.shard_map(shards, mesh=mesh, in_specs=in_specs, out_specs=out_specs, check_vma=False)
```

profile of v0, /device:TPU:0, one launch (start us, length us, event | category | flops | bytes accessed | tf_op | source)
XLA Modules:
  0.0 189.7 jit_solution(14777387597338560229)
XLA Ops:
  1.4 1.3 select_reduce_fusion.1
  3.4 23.3 %psum.14 = f32[2,4]{1,0:T(2,128)S(1)} all-reduce(f32[2,4]{1,0:T(2,128)S(1)} %and_select_fusion), channel_id=1, replica_groups=mesh['pair'=2,'seq'=4,'head'=4] {'pair','seq'}, use_global_device_ids=true, to_apply=%region_1.2 | all-reduce | flops 8 | bytes 64 | tf_op jit(solution)/shard_map/psum | solution.py:65
  26.6 0.8 select_reduce_fusion
  27.5 1.3 fusion.71
  31.6 0.9 fusion.84
  32.5 0.9 fusion.83
  33.4 1.2 fusion.70
  34.6 9.1 %all_gather.6 = bf16[1024,256]{1,0:T(8,128)(2,1)S(1)} all-gather(bf16[512,256]{1,0:T(8,128)(2,1)} %param.48), channel_id=1, replica_groups=mesh['pair'=2,'seq'=4,'head'=4] {'pair'}, dimensions={0}, use_global_device_ids=true | all-gather | bytes 786432 | tf_op jit(solution)/shard_map/all_gather | solution.py:76
  43.7 7.0 %all_gather.7 = bf16[1024,256]{1,0:T(8,128)(2,1)S(1)} all-gather(bf16[512,256]{1,0:T(8,128)(2,1)S(1)} %copy-done.13), channel_id=1, replica_groups=mesh['pair'=2,'seq'=4,'head'=4] {'pair'}, dimensions={0}, use_global_device_ids=true | all-gather | bytes 786432 | tf_op jit(solution)/shard_map/all_gather | solution.py:77
  51.7 0.8 pad_maximum_fusion.5
  53.3 1.6 conditional.5
  54.0 0.9 broadcast.478
  54.9 9.7 %conditional.6 = (bf16[512,128]{1,0:T(8,128)(2,1)S(1)}, f32[1024,128]{1,0:T(8,128)}, f32[1024,128]{1,0:T(8,128)S(1)}, f32[256,128]{1,0:T(8,128)S(1)}, f32[256,128]{1,0:T(8,128)S(1)}) conditional(s32[]{:T(128)} %convert_element_type.114, () %tuple.112, (s32[]{:T(128)}, bf16[256,1024]{1,0:T(8,128)(2,1)}, bf16[1152,128]{1,0:T(8,128)(2,1)}, ...), branch_computations={%region_15.16_spmd, %region_16.20_spmd} | conditional | flops 915430400 | bytes 28474960 | solution.py:114
  55.6 0.9 slice.276
  56.6 0.9 slice.277
  57.8 1.8 fusion.76
  63.7 0.8 slice.336
  65.3 1.0 pad_maximum_fusion.10
  66.3 0.9 reshape.380
  67.2 1.5 add_convert_fusion.2
  68.7 1.9 slice_add_fusion.2
  71.3 0.9 slice_add_fusion
  72.1 8.3 %conditional.4 = (bf16[512,128]{1,0:T(8,128)(2,1)S(1)}, f32[1024,128]{1,0:T(8,128)}, f32[1024,128]{1,0:T(8,128)S(1)}, f32[256,128]{1,0:T(8,128)S(1)}, f32[256,128]{1,0:T(8,128)S(1)}) conditional(s32[]{:T(128)} %convert_element_type.114, () %tuple.108, (s32[]{:T(128)}, bf16[256,1024]{1,0:T(8,128)(2,1)}, bf16[1152,128]{1,0:T(8,128)(2,1)S(1)}, ...), branch_computations={%region_5.6_spmd, %region_6.10_spmd} | conditional | flops 915430400 | bytes 27295284 | solution.py:114
  72.8 0.9 slice.266
  73.9 0.9 slice.267
  75.0 0.8 fusion.74
  79.5 0.8 slice.332
  81.2 1.0 pad_maximum_fusion.9
  82.4 0.9 maximum_bitcast_fusion
  83.3 1.0 add_convert_fusion.3
  84.3 1.3 slice_add_fusion.3
  86.5 101.7 %all-reduce.7 = bf16[1024,512]{1,0:T(8,128)(2,1)S(1)} all-reduce(f32[1024,512]{1,0:T(8,128)S(1)} %pad_maximum_fusion), channel_id=1, replica_groups=mesh['pair'=2,'seq'=4,'head'=4] {'pair','seq'}, use_global_device_ids=true, to_apply=%region_25.26 | all-reduce | flops 524288 | bytes 3145728 | tf_op jit(solution)/shard_map/psum | solution.py:131
  (93 shorter events, 19.9 us)
Async XLA Ops:
  0.6 43.1 %copy-start.13 = (bf16[512,256]{1,0:T(8,128)(2,1)S(1)}, bf16[512,256]{1,0:T(8,128)(2,1)}, u32[]{:S(2)}) copy-start(bf16[512,256]{1,0:T(8,128)(2,1)} %param.49) | copy-start | bytes 786436
  34.6 18.7 %copy-start = (bf16[256,1024]{1,0:T(8,128)(2,1)}, bf16[256,1024]{1,0:T(8,128)(2,1)S(1)}, u32[]{:S(2)}) copy-start(bf16[256,1024]{1,0:T(8,128)(2,1)S(1)} %fusion.70) | copy-start | bytes 1572868
  61.7 1.0 copy-start.5
  64.7 0.6 copy-start.7
  64.7 0.7 copy-start.11
  64.7 6.6 %copy-start.4 = (bf16[1152,128]{1,0:T(8,128)(2,1)S(1)}, bf16[1152,128]{1,0:T(8,128)(2,1)}, u32[]{:S(2)}) copy-start(bf16[1152,128]{1,0:T(8,128)(2,1)} %get-tuple-element.317) | copy-start | bytes 884740
  72.1 10.3 %copy-start.6 = (bf16[256,512]{1,0:T(8,128)(2,1)S(1)}, bf16[256,512]{1,0:T(8,128)(2,1)}, u32[]{:S(2)}) copy-start(bf16[256,512]{1,0:T(8,128)(2,1)} %reshape.380) | copy-start | bytes 786436
  80.5 0.6 copy-start.8
  80.5 0.7 copy-start.10
  80.5 0.7 copy-start.12
  80.5 5.0 %copy-start.15 = (bf16[256,128]{1,0:T(8,128)(2,1)S(1)}, bf16[256,128]{1,0:T(8,128)(2,1)}, u32[]{:S(2)}) copy-start(bf16[256,128]{1,0:T(8,128)(2,1)} %add_convert_fusion.2) | copy-start | bytes 196612
  81.2 5.0 %copy-start.9 = (f32[256,128]{1,0:T(8,128)S(1)}, f32[256,128]{1,0:T(8,128)}, u32[]{:S(2)}) copy-start(f32[256,128]{1,0:T(8,128)} %copy-done.8) | copy-start | bytes 393220
  82.4 3.9 %copy-start.1 = (f32[1024,128]{1,0:T(8,128)S(1)}, f32[1024,128]{1,0:T(8,128)}, u32[]{:S(2)}) copy-start(f32[1024,128]{1,0:T(8,128)} %slice_add_fusion.2) | copy-start | bytes 1572868
  82.4 3.9 %copy-start.2 = (f32[1024,128]{1,0:T(8,128)S(1)}, f32[1024,128]{1,0:T(8,128)}, u32[]{:S(2)}) copy-start(f32[1024,128]{1,0:T(8,128)} %slice_add_fusion) | copy-start | bytes 1572868
  86.5 101.8 %copy-start.14 = (bf16[256,128]{1,0:T(8,128)(2,1)S(1)}, bf16[256,128]{1,0:T(8,128)(2,1)}, u32[]{:S(2)}) copy-start(bf16[256,128]{1,0:T(8,128)(2,1)} %add_convert_fusion) | copy-start | bytes 196612
where the time goes:
time: 190 us
  blocking collectives  141 us (74%)
  other arithmetic  22.1 us (12%)
  local copies, waits for them, and re-layouts  15.6 us (8%)
  matrix products  7.8 us (4%)
  between operations  2.92 us (2%)
    psum x1, blocking collectives, shards(): summed = lax.psum(prompt_terms, ('pair', 'seq'))  102 us
    psum x1, blocking collectives, shards(): score_table = lax.psum(jnp.where(owned, own_sum, 0.0), ('pair', 'seq'))  23.3 us
    all_gather x1, blocking collectives, shards(): lax.all_gather(prompt_key, 'pair', axis=0, tiled=True)  9.08 us
    all_gather x1, blocking collectives, shards(): lax.all_gather(prompt_value, 'pair', axis=0, tiled=True)  7.04 us

commit v1 on v0

v1 whole, which is shorter than its diff:
```python
import functools
import math

import jax
import jax.numpy as jnp
from jax import lax
from jax.experimental import pallas as pl
from jax.experimental.pallas import tpu as pltpu
from jax.sharding import PartitionSpec as P

HEAD_DIM = 128
DPO_BETA = 0.1
MESH = pl.DeviceIdType.MESH
NT = (((1,), (1,)), ((), ()))
TN = (((0,), (0,)), ((), ()))
F32 = jnp.float32
BF16 = jnp.bfloat16


def dot_nt(a, b):
    return lax.dot_general(a, b, NT, preferred_element_type=F32)


def dot_tn(a, b):
    return lax.dot_general(a, b, TN, preferred_element_type=F32)


def kernel(
    n, lengths, partner, ratio, q_in, rk_in, rv_in, dir_in, pk_in, pv_in,
    qg_out, rkg_out, rvg_out, pkg_out, pvg_out,
    table, q_rows, g_rows, pk_far, pv_far, s_buf, dp_buf, ds_buf,
    x_send, x_recv, own_acc, z_send, z_recv, z_out,
    tab_send_sem, tab_recv_sem, kv_send_sem, kv_recv_sem,
    x_send_sem, x_recv_sem, rs_send_sem, rs_recv_sem, ag_send_sem, ag_recv_sem,
):
    rows = q_in.shape[2]
    half = pk_in.shape[0]
    kv_local = rk_in.shape[3] // HEAD_DIM
    group = q_in.shape[3] // rk_in.shape[3]
    lanes = rows * group
    piece = half // n
    block = min(256, half)
    blocks = half // block
    scale = 1.0 / math.sqrt(HEAD_DIM)
    exp_scale = scale * math.log2(math.e)
    side = lax.axis_index("pair")
    seq = lax.axis_index("seq")
    head = lax.axis_index("head")
    flat = side * n + seq
    pair_dev = (1 - side, seq, head)

    def peer(offset):
        other = lax.rem(flat + offset, 2 * n)
        return (other // n, lax.rem(other, n), head)

    def seq_peer(offset):
        return lax.rem(seq + offset, n)

    barrier = pltpu.get_barrier_semaphore()
    for d in range(1, 2 * n):
        pl.semaphore_signal(barrier, inc=1, device_id=peer(d), device_id_type=MESH)
    pl.semaphore_wait(barrier, 2 * n - 1)

    kv_copies = []
    for i in range(kv_local):
        cols = pl.ds(i * HEAD_DIM, HEAD_DIM)
        for which, (src, dst) in enumerate(((pk_in, pk_far), (pv_in, pv_far))):
            slot = 2 * i + which
            copy = pltpu.make_async_remote_copy(
                src_ref=src.at[:, cols], dst_ref=dst.at[i],
                send_sem=kv_send_sem.at[slot], recv_sem=kv_recv_sem.at[slot],
                device_id=pair_dev, device_id_type=MESH,
            )
            kv_copies.append(copy)

    length = lengths[0, 0]
    position = lax.broadcasted_iota(jnp.int32, (1, rows), 1)
    own_sum = jnp.sum(jnp.where(position < length, ratio[0], 0.0), axis=1, keepdims=True)
    table[flat] = jnp.broadcast_to(own_sum, (1, HEAD_DIM))
    tab_copies = []
    for d in range(1, 2 * n):
        copy = pltpu.make_async_remote_copy(
            src_ref=table.at[flat], dst_ref=table.at[flat],
            send_sem=tab_send_sem.at[d - 1], recv_sem=tab_recv_sem.at[d - 1],
            device_id=peer(d), device_id_type=MESH,
        )
        copy.start()
        tab_copies.append(copy)
    for copy in kv_copies:
        copy.start()

    for i in range(kv_local):
        for g in range(group):
            cols = slice((i * group + g) * HEAD_DIM, (i * group + g + 1) * HEAD_DIM)
            q_rows[i, g * rows:(g + 1) * rows, :] = q_in[0, 0, :, cols]

    def build_grads():
        for copy in tab_copies:
            copy.wait_recv()
        zero = jnp.zeros((1, HEAD_DIM), F32)
        mine = partner[seq]
        chosen, rejected = table[seq], zero
        chosen_r, rejected_r = zero, table[n + seq]
        for r in range(n):
            rejected = rejected + jnp.where(mine == r, table[n + r], 0.0)
            chosen_r = chosen_r + jnp.where(partner[r] == seq, table[r], 0.0)
        gap = jnp.where(side == 0, chosen - rejected, chosen_r - rejected_r)
        pulled = 1.0 / (1.0 + jnp.exp(DPO_BETA * gap))
        weight = jnp.where(side == 0, -pulled, pulled)
        live = lax.broadcasted_iota(jnp.int32, (rows, HEAD_DIM), 0) < length
        for i in range(kv_local):
            for g in range(group):
                cols = slice((i * group + g) * HEAD_DIM, (i * group + g + 1) * HEAD_DIM)
                value = weight * dir_in[0, 0, :, cols].astype(F32)
                g_rows[i, g * rows:(g + 1) * rows, :] = jnp.where(live, value, 0.0).astype(BF16)

    far_at, own_at, resp_at = 0, half, 2 * half

    def segments(i):
        cols = slice(i * HEAD_DIM, (i + 1) * HEAD_DIM)
        own = [
            (own_at + b * block, lambda b=b: pk_in[b * block:(b + 1) * block, cols],
             lambda b=b: pv_in[b * block:(b + 1) * block, cols])
            for b in range(blocks)
        ]
        resp = [(resp_at, lambda: rk_in[0, 0, :, cols], lambda: rv_in[0, 0, :, cols])]
        far = [
            (far_at + b * block, lambda b=b: pk_far[i, b * block:(b + 1) * block, :],
             lambda b=b: pv_far[i, b * block:(b + 1) * block, :])
            for b in range(blocks)
        ]
        return own, resp, far

    def score_block(i, at, keys, top, masked):
        scores = dot_nt(keys, q_rows[i])
        if masked:
            key_pos = lax.broadcasted_iota(jnp.int32, scores.shape, 0)
            row_pos = lax.rem(lax.broadcasted_iota(jnp.int32, scores.shape, 1), rows)
            scores = jnp.where((key_pos <= row_pos) & (key_pos < length), scores, -jnp.inf)
        s_buf[at:at + scores.shape[0], :] = scores
        return jnp.maximum(top, jnp.max(scores, axis=0, keepdims=True))

    def near_scores(i):
        own, resp, _ = segments(i)
        top = jnp.full((1, lanes), -jnp.inf, F32)
        for at, key, _v in own:
            top = score_block(i, at, key(), top, False)
        for at, key, _v in resp:
            top = score_block(i, at, key(), top, True)
        return top

    def far_scores(i, top):
        kv_copies[2 * i].wait_recv()
        for at, key, _v in segments(i)[2]:
            top = score_block(i, at, key(), top, False)
        return top

    def exp_pass(i, top):
        own, resp, far = segments(i)
        shift = top * exp_scale
        total = jnp.zeros((1, lanes), F32)
        delta = jnp.zeros((1, lanes), F32)
        for at, _k, value in own + resp + far:
            if at == far_at:
                kv_copies[2 * i + 1].wait_recv()
            v = value()
            span = slice(at, at + v.shape[0])
            e = jnp.exp2(s_buf[span, :] * exp_scale - shift)
            s_buf[span, :] = e
            dp = dot_nt(v, g_rows[i])
            dp_buf[span, :] = dp
            total = total + jnp.sum(e, axis=0, keepdims=True)
            delta = delta + jnp.sum(e * dp, axis=0, keepdims=True)
        inv = 1.0 / total
        return inv, delta * inv

    def grad_block(i, at, size, inv, delta):
        span = slice(at, at + size)
        prob = s_buf[span, :] * inv
        ds = (prob * (dp_buf[span, :] - delta)).astype(BF16)
        ds_buf[i, span, :] = ds
        dk = jnp.dot(ds, q_rows[i], preferred_element_type=F32) * scale
        dv = jnp.dot(prob.astype(BF16), g_rows[i], preferred_element_type=F32)
        return dk, dv

    def x_copy(i, b):
        slot = i * blocks + b
        return pltpu.make_async_remote_copy(
            src_ref=x_send.at[slot], dst_ref=x_recv.at[slot],
            send_sem=x_send_sem.at[slot], recv_sem=x_recv_sem.at[slot],
            device_id=pair_dev, device_id_type=MESH,
        )

    def grad_pass(i, inv, delta):
        for b in range(blocks):
            dk, dv = grad_block(i, far_at + b * block, block, inv, delta)
            x_send[i * blocks + b, :, :HEAD_DIM] = dk.astype(BF16)
            x_send[i * blocks + b, :, HEAD_DIM:] = dv.astype(BF16)
            x_copy(i, b).start()
        for b in range(blocks):
            dk, dv = grad_block(i, own_at + b * block, block, inv, delta)
            own_acc[i, b * block:(b + 1) * block, :HEAD_DIM] = dk
            own_acc[i, b * block:(b + 1) * block, HEAD_DIM:] = dv

    def resp_pass(i, inv, delta):
        dk, dv = grad_block(i, resp_at, rows, inv, delta)
        cols = slice(i * HEAD_DIM, (i + 1) * HEAD_DIM)
        rkg_out[0, 0, :, cols] = dk.astype(BF16)
        rvg_out[0, 0, :, cols] = dv.astype(BF16)

    def rs_copy(i, d):
        slot = i * (n - 1) + d - 1
        return pltpu.make_async_remote_copy(
            src_ref=z_send.at[i, seq_peer(d)], dst_ref=z_recv.at[slot],
            send_sem=rs_send_sem.at[slot], recv_sem=rs_recv_sem.at[slot],
            device_id=(side, seq_peer(d), head), device_id_type=MESH,
        )

    def ag_copy(i, d):
        slot = i * (n - 1) + d - 1
        return pltpu.make_async_remote_copy(
            src_ref=z_out.at[i, seq], dst_ref=z_out.at[i, seq],
            send_sem=ag_send_sem.at[slot], recv_sem=ag_recv_sem.at[slot],
            device_id=(side, seq_peer(d), head), device_id_type=MESH,
        )

    def start_rs(i):
        for b in range(blocks):
            x_copy(i, b).wait_recv()
        for p in range(n):
            b, at = p * piece // block, p * piece % block
            both = own_acc[i, p * piece:(p + 1) * piece, :] + x_recv[
                i * blocks + b, at:at + piece, :
            ].astype(F32)
            z_send[i, p] = both.astype(BF16)
        for d in range(1, n):
            rs_copy(i, d).start()

    def start_ag(i):
        total = z_send[i, seq].astype(F32)
        for d in range(1, n):
            rs_copy(i, d).wait_recv()
            total = total + z_recv[i * (n - 1) + d - 1].astype(F32)
        z_out[i, seq] = total.astype(BF16)
        for d in range(1, n):
            ag_copy(i, d).start()

    def finish(i):
        for d in range(1, n):
            ag_copy(i, d).wait_recv()
        cols = slice(i * HEAD_DIM, (i + 1) * HEAD_DIM)
        for p in range(n):
            at = slice(p * piece, (p + 1) * piece)
            pkg_out[at, cols] = z_out[i, p, :, :HEAD_DIM]
            pvg_out[at, cols] = z_out[i, p, :, HEAD_DIM:]

    def query_pass(i):
        own, resp, far = segments(i)
        total = jnp.zeros((HEAD_DIM, lanes), F32)
        for at, key, _v in own + resp + far:
            keys = key()
            total = total + dot_tn(keys, ds_buf[i, at:at + keys.shape[0], :])
        total = total * scale
        for g in range(group):
            cols = slice((i * group + g) * HEAD_DIM, (i * group + g + 1) * HEAD_DIM)
            qg_out[0, 0, :, cols] = total[:, g * rows:(g + 1) * rows].T.astype(BF16)

    for i in range(kv_local):
        top = near_scores(i)
        if i == 0:
            build_grads()
        top = far_scores(i, top)
        if i > 0:
            start_rs(i - 1)
        inv, delta = exp_pass(i, top)
        if i > 0:
            start_ag(i - 1)
        grad_pass(i, inv, delta)
        resp_pass(i, inv, delta)
    for i in range(kv_local - 1):
        query_pass(i)
    start_rs(kv_local - 1)
    query_pass(kv_local - 1)
    start_ag(kv_local - 1)
    for i in range(kv_local):
        finish(i)
    for copy in tab_copies + kv_copies:
        copy.wait_send()
    for i in range(kv_local):
        for b in range(blocks):
            x_copy(i, b).wait_send()
        for d in range(1, n):
            rs_copy(i, d).wait_send()
            ag_copy(i, d).wait_send()


def shards(
    n, resp_query, resp_key, resp_value, direction, ratio, lengths, partner, prompt_key, prompt_value
):
    rows = resp_query.shape[2]
    half, key_width = prompt_key.shape
    kv_local = key_width // HEAD_DIM
    lanes = rows * resp_query.shape[3] // key_width
    keys = 2 * half + rows
    piece = half // n
    block = min(256, half)
    blocks = half // block
    hops = max(kv_local * (n - 1), 1)
    vmem = pl.BlockSpec(memory_space=pltpu.VMEM)
    smem = pl.BlockSpec(memory_space=pltpu.SMEM)
    dma = pltpu.SemaphoreType.DMA
    return pl.pallas_call(
        functools.partial(kernel, n),
        out_shape=(
            jax.ShapeDtypeStruct(resp_query.shape, BF16),
            jax.ShapeDtypeStruct(resp_key.shape, BF16),
            jax.ShapeDtypeStruct(resp_value.shape, BF16),
            jax.ShapeDtypeStruct(prompt_key.shape, BF16),
            jax.ShapeDtypeStruct(prompt_value.shape, BF16),
        ),
        in_specs=[smem, smem] + [vmem] * 7,
        out_specs=(vmem,) * 5,
        scratch_shapes=[
            pltpu.VMEM((2 * n, 1, HEAD_DIM), F32),
            pltpu.VMEM((kv_local, lanes, HEAD_DIM), BF16),
            pltpu.VMEM((kv_local, lanes, HEAD_DIM), BF16),
            pltpu.VMEM((kv_local, half, HEAD_DIM), BF16),
            pltpu.VMEM((kv_local, half, HEAD_DIM), BF16),
            pltpu.VMEM((keys, lanes), F32),
            pltpu.VMEM((keys, lanes), F32),
            pltpu.VMEM((kv_local, keys, lanes), BF16),
            pltpu.VMEM((kv_local * blocks, block, 2 * HEAD_DIM), BF16),
            pltpu.VMEM((kv_local * blocks, block, 2 * HEAD_DIM), BF16),
            pltpu.VMEM((kv_local, half, 2 * HEAD_DIM), F32),
            pltpu.VMEM((kv_local, n, piece, 2 * HEAD_DIM), BF16),
            pltpu.VMEM((hops, piece, 2 * HEAD_DIM), BF16),
            pltpu.VMEM((kv_local, n, piece, 2 * HEAD_DIM), BF16),
            dma((2 * n - 1,)), dma((2 * n - 1,)),
            dma((2 * kv_local,)), dma((2 * kv_local,)),
            dma((kv_local * blocks,)), dma((kv_local * blocks,)),
            dma((hops,)), dma((hops,)), dma((hops,)), dma((hops,)),
        ],
        compiler_params=pltpu.CompilerParams(
            collective_id=0, has_side_effects=True, vmem_limit_bytes=60 * 1024 * 1024
        ),
        name="shared_prompt_backward",
    )(lengths, partner, ratio, resp_query, resp_key, resp_value, direction, prompt_key, prompt_value)


def solution(mesh):
    per_response = P("pair", "seq", None, "head")
    per_prompt = P("pair", "head")
    in_specs = (
        per_response, per_response, per_response, per_response,
        P("pair", "seq", None), P("pair", "seq"), P(), per_prompt, per_prompt,
    )
    out_specs = (per_response, per_response, per_response, per_prompt, per_prompt)
    return jax.shard_map(
        functools.partial(shards, mesh.shape["seq"]),
        mesh=mesh, in_specs=in_specs, out_specs=out_specs, check_vma=False,
    )
```

time: 190 us -> 61.9 us (0.33)
  blocking collectives: 141 us -> 0 us
  Pallas kernels: 0 us -> 55.4 us
  other arithmetic: 22.1 us -> 0 us
  local copies, waits for them, and re-layouts: 15.6 us -> 4.98 us
  matrix products: 7.8 us -> 0 us
    psum x2 -> x0, blocking collectives: 125 us -> none  [the longest x1 102 us: shards(): summed = lax.psum(prompt_terms, ('pair', 'seq'))]
    pallas_call x0 -> x1, Pallas kernels: none -> 55.4 us  [shards(): pl.pallas_call(functools.partial(kernel, n), out_shape=(jax.ShapeDtypeStr...]
    all_gather x2 -> x0, blocking collectives: 16.1 us -> none  [the longest x1 9.08 us: shards(): lax.all_gather(prompt_key, 'pair', axis=0, tiled=True)]
    slice x19 -> x0, local copies, waits for them, and re-layouts: 9.66 us -> none  [the longest x2 1.83 us: shards(): query_head[first_row:end_row].reshape(block_rows * head_group, HEAD_DIM)]
    dot_general x12 -> x0, matrix products: 7.8 us -> none  [the longest x2 2.66 us: block_pass(): jnp.dot(rows_q, key_rows.T, preferred_element_type=jnp.float32)]
    reduce_sum x5 -> x0, other arithmetic: 4.47 us -> none  [the longest x1 1.29 us: shards(): own_sum = jnp.sum(jnp.where(live_mask, ratio[0, 0], 0.0))]
    convert_element_type x5 -> x0, other arithmetic: 4.35 us -> none  [the longest x2 2.52 us: shards(): key_heads.append(resp_dk.astype(jnp.bfloat16))]
    add x4 -> x0, other arithmetic: 4.06 us -> none  [the longest x2 3.14 us: shards(): prompt_dk = prompt_dk + key_add[:prompt_rows]]
where the time goes in v1:
time: 61.9 us; the launch traced here: 61.7 us
  Pallas kernels  55.4 us (89%)
  local copies, waits for them, and re-layouts  4.98 us (8%)
  between operations  1.31 us (2%)
    pallas_call x1, Pallas kernels, shards(): pl.pallas_call(functools.partial(kernel, n), out_shape=(jax.ShapeDtypeStr...  55.4 us
    unnamed x13, local copies, waits for them, and re-layouts  4.98 us

profile of v1, /device:TPU:0, one launch (start us, length us, event | category | flops | bytes accessed | tf_op | source)
XLA Modules:
  0.0 61.7 jit_solution(17813442209861928065)
XLA Ops:
  1.3 55.4 %shared_prompt_backward.1 = (bf16[1,1,256,1024]{3,2,1,0:T(8,128)(2,1)}, bf16[1,1,256,256]{3,2,1,0:T(8,128)(2,1)}, bf16[1,1,256,256]{3,2,1,0:T(8,128)(2,1)}, bf16[512,256]{1,0:T(8,128)(2,1)}, bf16[512,256]{1,0:T(8,128)(2,1)}) custom-call(s32[1,1]{1,0:T(1,128)S(6)} %copy.19.lengths, s32[4]{0:T(128)} %partner.1, f32[1,1,256]{2,1,0:T(1,128)} %ratio.1, ...), custom_call_target="tpu_custom_call" | custom-call | tf_op jit(solution)/shard_map/shared_prompt_backward/pallas_call | solution.py:312
  56.7 0.0 copy-start.3
  56.7 0.0 copy-start.2
  56.7 1.9 %copy.20 = bf16[1,1,256,1024]{3,2,1,0:T(8,128)(2,1)} copy(bf16[1,1,256,1024]{3,2,1,0:T(8,128)(2,1)} %get-tuple-element.10) | data formatting | bytes 1048576
  58.6 0.0 copy-done.3
  58.6 0.0 copy-start.1
  58.6 0.7 %copy.21 = bf16[1,1,256,256]{3,2,1,0:T(8,128)(2,1)} copy(bf16[1,1,256,256]{3,2,1,0:T(8,128)(2,1)S(1)} %copy-done.3) | data formatting | bytes 262144
  59.3 0.0 copy-done.2
  59.3 0.7 %copy.22 = bf16[1,1,256,256]{3,2,1,0:T(8,128)(2,1)} copy(bf16[1,1,256,256]{3,2,1,0:T(8,128)(2,1)S(1)} %copy-done.2) | data formatting | bytes 262144
  59.9 0.0 copy-done.1
  59.9 0.0 copy-start
  59.9 0.7 %copy.23 = bf16[512,256]{1,0:T(8,128)(2,1)} copy(bf16[512,256]{1,0:T(8,128)(2,1)S(1)} %copy-done.1) | data formatting | bytes 524288
  60.7 0.3 copy-done
  61.0 0.7 %copy.24 = bf16[512,256]{1,0:T(8,128)(2,1)} copy(bf16[512,256]{1,0:T(8,128)(2,1)S(1)} %copy-done) | data formatting | bytes 524288
Async XLA Ops:
  56.7 1.9 %copy-start.3 = (bf16[1,1,256,256]{3,2,1,0:T(8,128)(2,1)S(1)}, bf16[1,1,256,256]{3,2,1,0:T(8,128)(2,1)}, u32[]{:S(2)}) copy-start(bf16[1,1,256,256]{3,2,1,0:T(8,128)(2,1)} %get-tuple-element.11) | copy-start | bytes 393220
  56.7 2.6 %copy-start.2 = (bf16[1,1,256,256]{3,2,1,0:T(8,128)(2,1)S(1)}, bf16[1,1,256,256]{3,2,1,0:T(8,128)(2,1)}, u32[]{:S(2)}) copy-start(bf16[1,1,256,256]{3,2,1,0:T(8,128)(2,1)} %get-tuple-element.12) | copy-start | bytes 393220
  58.6 1.3 %copy-start.1 = (bf16[512,256]{1,0:T(8,128)(2,1)S(1)}, bf16[512,256]{1,0:T(8,128)(2,1)}, u32[]{:S(2)}) copy-start(bf16[512,256]{1,0:T(8,128)(2,1)} %get-tuple-element.13) | copy-start | bytes 786436
  59.9 1.0 %copy-start = (bf16[512,256]{1,0:T(8,128)(2,1)S(1)}, bf16[512,256]{1,0:T(8,128)(2,1)}, u32[]{:S(2)}) copy-start(bf16[512,256]{1,0:T(8,128)(2,1)} %get-tuple-element.14) | copy-start | bytes 786436

commit v2 on v1

v2 whole, which is shorter than its diff:
```python
import functools
import math

import jax
import jax.numpy as jnp
from jax import lax
from jax.experimental import pallas as pl
from jax.experimental.pallas import tpu as pltpu
from jax.sharding import PartitionSpec as P

HEAD_DIM = 128
DPO_BETA = 0.1
BLOCK = 256
UNIT = 128
MESH = pl.DeviceIdType.MESH
NT = (((1,), (1,)), ((), ()))
TN = (((0,), (0,)), ((), ()))
F32 = jnp.float32
BF16 = jnp.bfloat16


def dot_nt(a, b):
    return lax.dot_general(a, b, NT, preferred_element_type=F32)


def dot_tn(a, b):
    return lax.dot_general(a, b, TN, preferred_element_type=F32)


def kernel(
    n, lengths, partner, ratio, q_in, rk_in, rv_in, dir_in, pk_in, pv_in,
    qg_out, rkg_out, rvg_out, pkg_out, pvg_out,
    table, q_rows, g_rows, pk_far, pv_far, s_buf, dp_buf, ds_buf,
    x_send, x_recv, own_acc, c_send, c_recv,
    tab_send_sem, tab_recv_sem, kv_send_sem, kv_recv_sem,
    x_send_sem, x_recv_sem, c_send_sem, c_recv_sem,
):
    rows = q_in.shape[2]
    half = pk_in.shape[0]
    kv_local = rk_in.shape[3] // HEAD_DIM
    group = q_in.shape[3] // rk_in.shape[3]
    lanes = rows * group
    block = min(BLOCK, half)
    blocks = half // block
    unit = min(UNIT, block)
    units = half // unit
    scale = 1.0 / math.sqrt(HEAD_DIM)
    exp_scale = scale * math.log2(math.e)
    side = lax.axis_index("pair")
    seq = lax.axis_index("seq")
    head = lax.axis_index("head")
    flat = side * n + seq
    pair_dev = (1 - side, seq, head)

    def peer(offset):
        other = lax.rem(flat + offset, 2 * n)
        return (other // n, lax.rem(other, n), head)

    def seq_peer(offset):
        return lax.rem(seq + offset, n)

    barrier = pltpu.get_barrier_semaphore()
    for d in range(1, 2 * n):
        pl.semaphore_signal(barrier, inc=1, device_id=peer(d), device_id_type=MESH)

    kv_copies = []
    for i in range(kv_local):
        cols = pl.ds(i * HEAD_DIM, HEAD_DIM)
        for which, (src, dst) in enumerate(((pk_in, pk_far), (pv_in, pv_far))):
            slot = 2 * i + which
            copy = pltpu.make_async_remote_copy(
                src_ref=src.at[:, cols], dst_ref=dst.at[i],
                send_sem=kv_send_sem.at[slot], recv_sem=kv_recv_sem.at[slot],
                device_id=pair_dev, device_id_type=MESH,
            )
            kv_copies.append(copy)

    length = lengths[0, 0]
    position = lax.broadcasted_iota(jnp.int32, (1, rows), 1)
    own_sum = jnp.sum(jnp.where(position < length, ratio[0], 0.0), axis=1, keepdims=True)
    table[flat] = jnp.broadcast_to(own_sum, (1, HEAD_DIM))
    tab_copies = []

    def build_grads():
        for copy in tab_copies:
            copy.wait_recv()
        zero = jnp.zeros((1, HEAD_DIM), F32)
        mine = partner[seq]
        chosen, rejected = table[seq], zero
        chosen_r, rejected_r = zero, table[n + seq]
        for r in range(n):
            rejected = rejected + jnp.where(mine == r, table[n + r], 0.0)
            chosen_r = chosen_r + jnp.where(partner[r] == seq, table[r], 0.0)
        gap = jnp.where(side == 0, chosen - rejected, chosen_r - rejected_r)
        pulled = 1.0 / (1.0 + jnp.exp(DPO_BETA * gap))
        weight = jnp.where(side == 0, -pulled, pulled)
        live = lax.broadcasted_iota(jnp.int32, (rows, HEAD_DIM), 0) < length
        for i in range(kv_local):
            for g in range(group):
                cols = slice((i * group + g) * HEAD_DIM, (i * group + g + 1) * HEAD_DIM)
                value = weight * dir_in[0, 0, :, cols].astype(F32)
                g_rows[i, g * rows:(g + 1) * rows, :] = jnp.where(live, value, 0.0).astype(BF16)

    far_at, own_at, resp_at = 0, half, 2 * half

    def segments(i):
        cols = slice(i * HEAD_DIM, (i + 1) * HEAD_DIM)
        own = [
            (own_at + b * block, lambda b=b: pk_in[b * block:(b + 1) * block, cols],
             lambda b=b: pv_in[b * block:(b + 1) * block, cols])
            for b in range(blocks)
        ]
        resp = [(resp_at, lambda: rk_in[0, 0, :, cols], lambda: rv_in[0, 0, :, cols])]
        far = [
            (far_at + b * block, lambda b=b: pk_far[i, b * block:(b + 1) * block, :],
             lambda b=b: pv_far[i, b * block:(b + 1) * block, :])
            for b in range(blocks)
        ]
        return own, resp, far

    def score_block(i, at, keys, top, masked):
        scores = dot_nt(keys, q_rows[i])
        if masked:
            key_pos = lax.broadcasted_iota(jnp.int32, scores.shape, 0)
            row_pos = lax.rem(lax.broadcasted_iota(jnp.int32, scores.shape, 1), rows)
            scores = jnp.where((key_pos <= row_pos) & (key_pos < length), scores, -jnp.inf)
        s_buf[i, at:at + scores.shape[0], :] = scores
        return jnp.maximum(top, jnp.max(scores, axis=0, keepdims=True))

    def near_scores(i):
        own, resp, _ = segments(i)
        top = jnp.full((1, lanes), -jnp.inf, F32)
        for at, key, _v in own:
            top = score_block(i, at, key(), top, False)
        for at, key, _v in resp:
            top = score_block(i, at, key(), top, True)
        return top

    def far_scores(i, top):
        kv_copies[2 * i].wait_recv()
        for at, key, _v in segments(i)[2]:
            top = score_block(i, at, key(), top, False)
        return top

    def prob_grad_block(i, at, v):
        dp_buf[i, at:at + v.shape[0], :] = dot_nt(v, g_rows[i])

    def near_prob_grads(i):
        own, resp, _ = segments(i)
        for at, _k, value in own + resp:
            prob_grad_block(i, at, value())

    def exp_pass(i, top):
        own, resp, far = segments(i)
        shift = top * exp_scale
        total = jnp.zeros((1, lanes), F32)
        delta = jnp.zeros((1, lanes), F32)
        for at, _k, value in own + resp + far:
            if at == far_at:
                kv_copies[2 * i + 1].wait_recv()
            span = slice(at, at + (rows if at == resp_at else block))
            if at < own_at:
                prob_grad_block(i, at, value())
            e = jnp.exp2(s_buf[i, span, :] * exp_scale - shift)
            s_buf[i, span, :] = e
            total = total + jnp.sum(e, axis=0, keepdims=True)
            delta = delta + jnp.sum(e * dp_buf[i, span, :], axis=0, keepdims=True)
        inv = 1.0 / total
        return inv, delta * inv

    def grad_block(i, at, size, inv, delta):
        span = slice(at, at + size)
        prob = s_buf[i, span, :] * inv
        ds = (prob * (dp_buf[i, span, :] - delta)).astype(BF16)
        ds_buf[i, span, :] = ds
        dk = jnp.dot(ds, q_rows[i], preferred_element_type=F32) * scale
        dv = jnp.dot(prob.astype(BF16), g_rows[i], preferred_element_type=F32)
        return dk, dv

    def x_copy(u):
        return pltpu.make_async_remote_copy(
            src_ref=x_send.at[u], dst_ref=x_recv.at[u],
            send_sem=x_send_sem.at[u], recv_sem=x_recv_sem.at[u],
            device_id=pair_dev, device_id_type=MESH,
        )

    def far_pass(i, inv, delta):
        for b in range(blocks):
            dk, dv = grad_block(i, far_at + b * block, block, inv, delta)
            for k in range(block // unit):
                u = i * units + b * (block // unit) + k
                x_send[u, :, :HEAD_DIM] = dk[k * unit:(k + 1) * unit].astype(BF16)
                x_send[u, :, HEAD_DIM:] = dv[k * unit:(k + 1) * unit].astype(BF16)
                x_copy(u).start()

    def own_pass(i, inv, delta):
        for b in range(blocks):
            dk, dv = grad_block(i, own_at + b * block, block, inv, delta)
            own_acc[i, b * block:(b + 1) * block, :HEAD_DIM] = dk
            own_acc[i, b * block:(b + 1) * block, HEAD_DIM:] = dv

    def resp_pass(i, inv, delta):
        dk, dv = grad_block(i, resp_at, rows, inv, delta)
        cols = slice(i * HEAD_DIM, (i + 1) * HEAD_DIM)
        rkg_out[0, 0, :, cols] = dk.astype(BF16)
        rvg_out[0, 0, :, cols] = dv.astype(BF16)

    def chain_copy(u, way):
        turn = (1 - way) // 2
        return pltpu.make_async_remote_copy(
            src_ref=c_send.at[2 * u + turn], dst_ref=c_recv.at[2 * u + turn],
            send_sem=c_send_sem.at[2 * u + turn], recv_sem=c_recv_sem.at[2 * u + turn],
            device_id=(side, lax.rem(seq + way + n, n), head), device_id_type=MESH,
        )

    first_way = jnp.where(2 * seq < n, 1, -1)

    def chain_step(u, i, at, way):
        has_from = (seq - way >= 0) & (seq - way < n)
        has_to = (seq + way >= 0) & (seq + way < n)
        turn = (1 - way) // 2

        @pl.when(has_from)
        def _():
            chain_copy(u, way).wait_recv()

        @pl.when(has_to & has_from)
        def _():
            passed = own_acc[i, at:at + unit, :] + c_recv[2 * u + turn].astype(F32)
            c_send[2 * u + turn] = passed.astype(BF16)

        @pl.when(has_to & jnp.logical_not(has_from))
        def _():
            c_send[2 * u + turn] = own_acc[i, at:at + unit, :].astype(BF16)

        @pl.when(has_to)
        def _():
            chain_copy(u, way).start()

    def chain(u):
        i, at = u // units, u % units * unit
        x_copy(u).wait_recv()
        own_acc[i, at:at + unit, :] += x_recv[u].astype(F32)
        chain_step(u, i, at, first_way)

    def chain_back(u):
        i, at = u // units, u % units * unit
        chain_step(u, i, at, -first_way)
        cols = slice(i * HEAD_DIM, (i + 1) * HEAD_DIM)

        for way in (1, -1):
            @pl.when((seq - way >= 0) & (seq - way < n))
            def _():
                own_acc[i, at:at + unit, :] += c_recv[2 * u + (1 - way) // 2].astype(F32)
        pkg_out[at:at + unit, cols] = own_acc[i, at:at + unit, :HEAD_DIM].astype(BF16)
        pvg_out[at:at + unit, cols] = own_acc[i, at:at + unit, HEAD_DIM:].astype(BF16)

    def query_pass(i):
        own, resp, far = segments(i)
        total = jnp.zeros((HEAD_DIM, lanes), F32)
        for at, key, _v in own + resp + far:
            keys = key()
            total = total + dot_tn(keys, ds_buf[i, at:at + keys.shape[0], :])
        total = total * scale
        for g in range(group):
            cols = slice((i * group + g) * HEAD_DIM, (i * group + g + 1) * HEAD_DIM)
            qg_out[0, 0, :, cols] = total[:, g * rows:(g + 1) * rows].T.astype(BF16)

    count = kv_local * units
    for i in range(kv_local):
        for g in range(group):
            cols = slice((i * group + g) * HEAD_DIM, (i * group + g + 1) * HEAD_DIM)
            q_rows[i, g * rows:(g + 1) * rows, :] = q_in[0, 0, :, cols]
    tops = [near_scores(0)]
    pl.semaphore_wait(barrier, 2 * n - 1)
    for d in range(1, 2 * n):
        copy = pltpu.make_async_remote_copy(
            src_ref=table.at[flat], dst_ref=table.at[flat],
            send_sem=tab_send_sem.at[d - 1], recv_sem=tab_recv_sem.at[d - 1],
            device_id=peer(d), device_id_type=MESH,
        )
        copy.start()
        tab_copies.append(copy)
    for copy in kv_copies:
        copy.start()
    tops += [near_scores(i) for i in range(1, kv_local)]
    build_grads()
    for i in range(kv_local):
        near_prob_grads(i)
    stats = []
    for i in range(kv_local):
        stats.append(exp_pass(i, far_scores(i, tops[i])))
        far_pass(i, *stats[i])
        own_pass(i, *stats[i])
        if i > 0:
            for u in range((i - 1) * units, i * units):
                chain(u)
    for i in range(kv_local):
        resp_pass(i, *stats[i])
        query_pass(i)
    for u in range((kv_local - 1) * units, count):
        chain(u)
    for u in range(count):
        chain_back(u)
    for copy in tab_copies + kv_copies:
        copy.wait_send()
    for u in range(count):
        x_copy(u).wait_send()
        for way in (1, -1):
            @pl.when((seq + way >= 0) & (seq + way < n))
            def _():
                chain_copy(u, way).wait_send()


def store_kernel(count, *refs):
    sources, targets, held = refs[:count], refs[count:2 * count], refs[2 * count:3 * count]
    in_sem, out_sem = refs[3 * count:]
    loads = [
        pltpu.make_async_copy(sources[k], held[k], in_sem.at[k]) for k in range(count)
    ]
    stores = [
        pltpu.make_async_copy(held[k], targets[k], out_sem.at[k]) for k in range(count)
    ]
    for load in loads:
        load.start()
    for load, store in zip(loads, stores):
        load.wait()
        store.start()
    for store in stores:
        store.wait()


def store_all(arrays):
    count = len(arrays)
    return pl.pallas_call(
        functools.partial(store_kernel, count),
        out_shape=tuple(jax.ShapeDtypeStruct(a.shape, a.dtype) for a in arrays),
        in_specs=[pl.BlockSpec(memory_space=pl.ANY)] * count,
        out_specs=(pl.BlockSpec(memory_space=pl.ANY),) * count,
        scratch_shapes=[pltpu.VMEM(a.shape, a.dtype) for a in arrays]
        + [pltpu.SemaphoreType.DMA((count,)), pltpu.SemaphoreType.DMA((count,))],
        name="store_results",
    )(*arrays)


def shards(
    n, resp_query, resp_key, resp_value, direction, ratio, lengths, partner, prompt_key, prompt_value
):
    rows = resp_query.shape[2]
    half, key_width = prompt_key.shape
    kv_local = key_width // HEAD_DIM
    lanes = rows * resp_query.shape[3] // key_width
    keys = 2 * half + rows
    block = min(BLOCK, half)
    blocks = half // block
    unit = min(UNIT, block)
    count = kv_local * (half // unit)
    vmem = pl.BlockSpec(memory_space=pltpu.VMEM)
    smem = pl.BlockSpec(memory_space=pltpu.SMEM)
    dma = pltpu.SemaphoreType.DMA
    results = pl.pallas_call(
        functools.partial(kernel, n),
        out_shape=(
            jax.ShapeDtypeStruct(resp_query.shape, BF16),
            jax.ShapeDtypeStruct(resp_key.shape, BF16),
            jax.ShapeDtypeStruct(resp_value.shape, BF16),
            jax.ShapeDtypeStruct(prompt_key.shape, BF16),
            jax.ShapeDtypeStruct(prompt_value.shape, BF16),
        ),
        in_specs=[smem, smem] + [vmem] * 7,
        out_specs=(vmem,) * 5,
        scratch_shapes=[
            pltpu.VMEM((2 * n, 1, HEAD_DIM), F32),
            pltpu.VMEM((kv_local, lanes, HEAD_DIM), BF16),
            pltpu.VMEM((kv_local, lanes, HEAD_DIM), BF16),
            pltpu.VMEM((kv_local, half, HEAD_DIM), BF16),
            pltpu.VMEM((kv_local, half, HEAD_DIM), BF16),
            pltpu.VMEM((kv_local, keys, lanes), F32),
            pltpu.VMEM((kv_local, keys, lanes), F32),
            pltpu.VMEM((kv_local, keys, lanes), BF16),
            pltpu.VMEM((count, unit, 2 * HEAD_DIM), BF16),
            pltpu.VMEM((count, unit, 2 * HEAD_DIM), BF16),
            pltpu.VMEM((kv_local, half, 2 * HEAD_DIM), F32),
            pltpu.VMEM((2 * count, unit, 2 * HEAD_DIM), BF16),
            pltpu.VMEM((2 * count, unit, 2 * HEAD_DIM), BF16),
            dma((2 * n - 1,)), dma((2 * n - 1,)),
            dma((2 * kv_local,)), dma((2 * kv_local,)),
            dma((count,)), dma((count,)),
            dma((2 * count,)), dma((2 * count,)),
        ],
        compiler_params=pltpu.CompilerParams(
            collective_id=0, has_side_effects=True, vmem_limit_bytes=60 * 1024 * 1024
        ),
        name="shared_prompt_backward",
    )(lengths, partner, ratio, resp_query, resp_key, resp_value, direction, prompt_key, prompt_value)
    return store_all(results)


def solution(mesh):
    per_response = P("pair", "seq", None, "head")
    per_prompt = P("pair", "head")
    in_specs = (
        per_response, per_response, per_response, per_response,
        P("pair", "seq", None), P("pair", "seq"), P(), per_prompt, per_prompt,
    )
    out_specs = (per_response, per_response, per_response, per_prompt, per_prompt)
    return jax.shard_map(
        functools.partial(shards, mesh.shape["seq"]),
        mesh=mesh, in_specs=in_specs, out_specs=out_specs, check_vma=False,
    )
```

time: 61.9 us -> 52.2 us (0.84)
  local copies, waits for them, and re-layouts: 4.98 us -> 0 us
  Pallas kernels: 55.4 us -> 50.7 us
    pallas_call x1, Pallas kernels: 55.4 us -> 48.5 us  [shards(): pl.pallas_call(functools.partial(kernel, n), out_shape=(jax.ShapeDtypeStr...]
    unnamed x13 -> x0, local copies, waits for them, and re-layouts: 4.98 us -> none
    pallas_call x0 -> x1, Pallas kernels: none -> 2.18 us  [store_all(): pl.pallas_call(functools.partial(store_kernel, count), out_shape=tuple((j...]
where the time goes in v2:
time: 52.2 us; the launch traced here: 52 us
  Pallas kernels  50.7 us (97%)
  between operations  1.29 us (2%)
    pallas_call x1, Pallas kernels, shards(): pl.pallas_call(functools.partial(kernel, n), out_shape=(jax.ShapeDtypeStr...  48.5 us
    pallas_call x1, Pallas kernels, store_all(): pl.pallas_call(functools.partial(store_kernel, count), out_shape=tuple((j...  2.18 us

profile of v2, /device:TPU:0, one launch (start us, length us, event | category | flops | bytes accessed | tf_op | source)
XLA Modules:
  0.0 52.0 jit_solution(9062010866715320942)
XLA Ops:
  1.3 48.5 %shared_prompt_backward.1 = (bf16[1,1,256,1024]{3,2,1,0:T(8,128)(2,1)}, bf16[1,1,256,256]{3,2,1,0:T(8,128)(2,1)}, bf16[1,1,256,256]{3,2,1,0:T(8,128)(2,1)}, bf16[512,256]{1,0:T(8,128)(2,1)}, bf16[512,256]{1,0:T(8,128)(2,1)}) custom-call(s32[1,1]{1,0:T(1,128)S(6)} %copy.14.lengths, s32[4]{0:T(128)} %partner.1, f32[1,1,256]{2,1,0:T(1,128)} %ratio.1, ...), custom_call_target="tpu_custom_call" | custom-call | tf_op jit(solution)/shard_map/shared_prompt_backward/pallas_call | solution.py:361
  49.8 2.2 %store_results.1 = (bf16[1,1,256,1024]{3,2,1,0:T(8,128)(2,1)}, bf16[1,1,256,256]{3,2,1,0:T(8,128)(2,1)}, bf16[1,1,256,256]{3,2,1,0:T(8,128)(2,1)}, bf16[512,256]{1,0:T(8,128)(2,1)}, bf16[512,256]{1,0:T(8,128)(2,1)}) custom-call(bf16[1,1,256,1024]{3,2,1,0:T(8,128)(2,1)} %get-tuple-element.10.refs_0_, bf16[1,1,256,256]{3,2,1,0:T(8,128)(2,1)} %get-tuple-element.11.refs_1_, ...), custom_call_target="tpu_custom_call" | custom-call | tf_op jit(solution)/shard_map/store_results/pallas_call | solution.py:335
